TPU v7x, 32 devices: a whole 2x2x4 slice. The times are simulated.
32 devices in a mesh: ex: 16 (over z, x, core), feat: 2 (over y).
Axes of the slice: x: 2, y: 2, z: 4, core: 2. Of those that a mesh axis runs over, the one named last changes fastest.
Arguments:
- lanczos_basis: bfloat16 [131072, 384], P(('ex', 'feat')), may hold values from -0.3125 to 0.3125
- diagonal: float32 [131072], P(('ex', 'feat')), may hold values from 0.3 to 9
- lanczos_scale: float32 [384], replicated, may hold values from 0.3 to 3
- test_tiles: int32 [64, 16], replicated, may hold values from 0 to 1023, as said below
- test_values: bfloat16 [64, 16, 128], replicated, may hold values from -6 to 6
- train_tiles: int32 [256, 16], P('ex', 'feat'), may hold values from 0 to 1023, as said below
- train_count: int32 [256, 2], P('ex', 'feat'), may hold values from 1 to 8, as said below
- train_values: bfloat16 [256, 16, 16, 128], P('ex', 'feat'), may hold values from -6 to 6
- resid_weight: float32 [4096], P('ex'), may hold values from -1 to 1
Outputs:
- influence: float32 [64, 4096], P('feat', 'ex')
Inputs may be any that keep to these rules, and one draw needn't show every extreme that they name: `train_tiles`: tile id j lies in the basis rows of the device whose index along ex+feat (ex slowest) is j // 32; the ids in slots f * 8 to (f + 1) * 8 - 1 of a block lie in rows of devices with feat index f. Among all slots of the blocks of one index of ex on one index of feat, at most 12 ids lie in the rows of any one device. In every draw, for each feat index, some device has 12 live slots naming its rows in the blocks of every index of ex. `train_count`: in every draw some block of every index of ex has all 8 slots live on every index of feat. `test_tiles`: the tile ids of one test example are distinct.
All inputs are finite; a program needn't handle non-finite values.
Results may differ from a plain program's by a relative error of at most 0.0042.
Values may be sent and summed in bfloat16 or wider, within the bound.
No kernel may reach another device: no remote copies, remote signals or barrier semaphores. Data moves between devices by JAX's collectives and lax.ppermute only.
A program may use at most 64 MiB of HBM per device.

v0:
```python
import jax
import jax.numpy as jnp
from jax import lax
from jax.sharding import PartitionSpec as P


def body(
    lanczos_basis,
    diagonal,
    lanczos_scale,
    test_tiles,
    test_values,
    train_tiles,
    train_count,
    train_values,
    resid_weight,
):
    ex_devices = lax.axis_size("ex")
    feat_devices = lax.axis_size("feat")
    feat_rows = lanczos_basis.shape[0]
    tiles_here = feat_rows // 128
    test_count = test_tiles.shape[0]
    ex_index = lax.axis_index("ex")
    feat_index = lax.axis_index("feat")
    first_tile = (ex_index * feat_devices + feat_index) * tiles_here
    offsets = test_tiles - first_tile
    matches = (offsets[None, :, :] == jnp.arange(tiles_here)[:, None, None]).astype(jnp.bfloat16)
    local_test = jnp.einsum(
        "ats,tsf->atf", matches, test_values, preferred_element_type=jnp.float32
    ).astype(jnp.bfloat16)
    basis_tiles = lanczos_basis.reshape(tiles_here, 128, lanczos_basis.shape[1])
    partial_proj = jnp.einsum(
        "afr,atf->tr", basis_tiles, local_test, preferred_element_type=jnp.float32
    )
    diag_tiles = diagonal.reshape(tiles_here, 128)
    test_wide = local_test.astype(jnp.float32)
    projection = lax.psum(partial_proj, ("ex", "feat"))
    scaled_proj = (lanczos_scale[None, :] * projection).astype(jnp.bfloat16)
    exact_dir = diag_tiles[:, None, :] * test_wide + jnp.einsum(
        "afr,tr->atf", basis_tiles, scaled_proj, preferred_element_type=jnp.float32
    )
    self_inf = lax.psum(jnp.sum(test_wide * exact_dir, axis=(0, 2)), ("ex", "feat"))
    direction = exact_dir.astype(jnp.bfloat16)
    blocks_here = train_tiles.shape[0]
    slots_here = train_tiles.shape[1]
    slot_total = blocks_here * slots_here
    capacity = max(2, (3 * slot_total + 2 * ex_devices - 1) // (2 * ex_devices))
    flat_ids = train_tiles.reshape(slot_total)
    owners = flat_ids // tiles_here // feat_devices
    local_tile = flat_ids % tiles_here
    slot_live = (jnp.arange(slots_here)[None, :] < train_count).reshape(slot_total)
    onehot = ((owners[:, None] == jnp.arange(ex_devices)[None, :]) & slot_live[:, None]).astype(
        jnp.int32
    )
    slot_rank = jnp.sum(onehot * (jnp.cumsum(onehot, axis=0) - 1), axis=1)
    targets = jnp.where(slot_live, owners, ex_devices)
    requests = (
        jnp.full((ex_devices, capacity), -1, jnp.int32)
        .at[targets, slot_rank]
        .set(local_tile, mode="drop")
    )
    fetched = direction[
        jnp.maximum(lax.all_to_all(requests, "ex", split_axis=0, concat_axis=0, tiled=True), 0)
    ]
    returned = lax.all_to_all(fetched, "ex", split_axis=0, concat_axis=0, tiled=True)
    gathered = jnp.where(
        slot_live[:, None, None], returned[owners, slot_rank], jnp.zeros((), jnp.bfloat16)
    )
    gathered = gathered.reshape(blocks_here, slots_here, test_count, 128)
    partial_scores = jnp.einsum(
        "bjef,bjtf->tbe", train_values, gathered, preferred_element_type=jnp.float32
    ).reshape(test_count, -1)
    tests_here = test_count // feat_devices
    own_scores = lax.psum_scatter(partial_scores, "feat", scatter_dimension=0, tiled=True)
    self_mine = lax.dynamic_slice_in_dim(self_inf, feat_index * tests_here, tests_here)
    return -resid_weight[None, :] * own_scores / jnp.sqrt(self_mine)[:, None]


def solution(mesh):
    return jax.shard_map(
        body,
        mesh=mesh,
        in_specs=(
            P(("ex", "feat"), None),
            P(("ex", "feat")),
            P(),
            P(),
            P(),
            P("ex", "feat"),
            P("ex", "feat"),
            P("ex", "feat", None, None),
            P("ex"),
        ),
        out_specs=P("feat", "ex"),
        check_vma=False,
    )
```

profile of v0, /device:TPU:0, one launch (start us, length us, event | category | flops | bytes accessed | tf_op | source)
XLA Modules:
  0.0 305.9 jit_solution(2954951502102230224)
XLA Ops:
  6.5 0.0 copy-start
  6.5 0.0 copy-start.4
  6.5 0.9 copy.25
  7.4 0.1 reshape.251
  7.5 0.1 reshape.250
  7.6 0.7 iota_compare_fusion.3
  8.4 0.1 lt.83
  8.5 0.1 lt.81
  8.6 0.1 fusion.11
  8.7 0.2 reduce_window_sum.11
  8.9 0.2 select_reduce_fusion
  9.1 0.6 broadcast_in_dim.15
  9.7 18.5 %scatter_fusion = s32[16,12]{1,0:T(8,128)} fusion(s32[16,12]{1,0:T(8,128)} %broadcast_in_dim.15, s32[128]{0:T(128)S(1)} %fusion.21, s32[128]{0:T(128)S(1)} %get-tuple-element.9), kind=kCustom, calls=%fused_computation.2 | custom fusion | bytes 2560 | tf_op jit(solution)/shard_map/scatter | solution.py:60
  28.2 7.1 %all-to-all-start = ((s32[16,1,12]{2,1,0:T(1,128)}), s32[16,1,12]{2,1,0:T(1,128)S(1)}, u32[]{:S(2)}, u32[]{:S(2)}) async-start(s32[16,1,12]{2,1,0:T(1,128)} %bitcast.10), calls=%async_computation | async-start | bytes 16384 | tf_op jit(solution)/shard_map/all_to_all | solution.py:63
  35.3 0.0 all-reduce.2.cloned.1.call-start
  35.4 0.7 broadcast_subtract_fusion
  36.1 0.1 copy.22
  36.2 1.6 fusion.3
  37.8 0.0 copy-done
  37.8 0.0 copy-start.1
  37.8 0.8 copy-done.1
  38.6 1.3 convolution_bitcast_fusion
  39.8 0.0 copy-start.3
  39.8 0.0 all-reduce.2.cloned.1.call-update
  39.9 0.0 reduce-scatter.2.cloned.1.call-start
  39.9 1.8 all-to-all-done
  41.7 0.1 reshape.255
  41.8 124.3 %all-reduce.2.cloned.1.call-done = f32[64,384]{1,0:T(8,128)} async-done(((f32[64,384]{1,0:T(8,128)}), f32[64,384]{1,0:T(8,128)}) %all-reduce.2.cloned.1.call-update) | async-done | bytes 98320 | tf_op jit(solution)/shard_map/psum | solution.py:37
  166.1 0.0 copy-done.4
  166.1 0.0 copy-start.2
  166.1 2.0 fusion.13
  168.2 0.0 copy-done.3
  168.2 0.0 copy-done.2
  168.2 0.8 fusion.5
  169.0 1.0 copy.28
  170.0 3.8 %gather_fusion = bf16[192,64,128]{2,1,0:T(8,128)(2,1)} fusion(bf16[32,64,128]{2,1,0:T(8,128)(2,1)} %copy.28, s32[1024]{0:T(1024)S(1)} %pad_clamp_fusion), kind=kCustom, calls=%fused_computation | custom fusion | bytes 6292224 | tf_op jit(solution)/shard_map/gather | solution.py:62
  173.8 76.2 %all_to_all.14 = bf16[16,12,64,128]{3,2,1,0:T(8,128)(2,1)} all-to-all(bf16[16,12,64,128]{3,2,1,0:T(8,128)(2,1)} %bitcast.43), channel_id=1, replica_groups=mesh['ex'=16,'feat'=2] {'ex'}, dimensions={0} | all-to-all | bytes 6291456 | tf_op jit(solution)/shard_map/all_to_all | solution.py:65
  250.0 4.2 %gather_fusion.1 = bf16[128,64,128]{2,1,0:T(8,128)(2,1)} fusion(bf16[16,12,64,128]{3,2,1,0:T(8,128)(2,1)} %all_to_all.14, s32[128]{0:T(128)S(1)} %get-tuple-element.5), kind=kCustom, calls=%fused_computation.1 | custom fusion | bytes 4195328 | tf_op jit(solution)/shard_map/gather | solution.py:67
  254.2 0.0 copy-start.5
  254.2 2.4 fusion
  256.6 0.7 copy.29
  257.3 0.0 reduce-scatter.2.cloned.1.call-update
  257.4 0.0 copy-done.5
  257.4 40.1 %psum.15 = f32[64]{0:T(128)S(1)} all-reduce(f32[64]{0:T(128)S(1)} %get-tuple-element.7), channel_id=1, replica_groups=mesh['ex'=16,'feat'=2] {'ex','feat'}, use_global_device_ids=true, to_apply=%region_6.7 | all-reduce | flops 64 | bytes 512 | tf_op jit(solution)/shard_map/psum | solution.py:42
  297.5 0.1 dynamic-slice_sqrt_fusion
  297.6 0.0 reduce-scatter.2.cloned.1.call-done
  297.6 1.5 multiply_divide_fusion
  (6 shorter events, 0.1 us)
Async XLA Ops:
  6.5 31.2 %copy-start = (bf16[4096,384]{1,0:T(8,128)(2,1)S(1)}, bf16[4096,384]{1,0:T(8,128)(2,1)}, u32[]{:S(2)}) copy-start(bf16[4096,384]{1,0:T(8,128)(2,1)} %param.9) | copy-start | bytes 9437188
  6.5 159.6 %copy-start.4 = (f32[384]{0:T(512)S(1)}, f32[384]{0:T(512)}, u32[]{:S(2)}) copy-start(f32[384]{0:T(512)} %param.11) | copy-start | bytes 4612
  28.2 13.5 %all-to-all-start = ((s32[16,1,12]{2,1,0:T(1,128)}), s32[16,1,12]{2,1,0:T(1,128)S(1)}, u32[]{:S(2)}, u32[]{:S(2)}) async-start(s32[16,1,12]{2,1,0:T(1,128)} %bitcast.10), calls=%async_computation | async-start | bytes 16384 | tf_op jit(solution)/shard_map/all_to_all | solution.py:63
  35.3 130.8 %all-reduce.2.cloned.1.call-start = ((), (), s32[]{:S(2)}) async-start(), calls=%async_computation.3 | async-start | bytes 196608 | tf_op jit(solution)/shard_map/psum | solution.py:37
  37.8 0.8 copy-start.1
  39.8 128.4 %copy-start.3 = (f32[4096]{0:T(1024)S(1)}, f32[4096]{0:T(1024)}, u32[]{:S(2)}) copy-start(f32[4096]{0:T(1024)} %param.10) | copy-start | bytes 49156
  39.9 257.7 %reduce-scatter.2.cloned.1.call-start = ((), (), s32[]{:S(2)}) async-start(), calls=%async_computation.4 | async-start | bytes 98304 | tf_op jit(solution)/shard_map/reduce_scatter | solution.py:74
  166.1 2.1 copy-start.2
  254.2 3.1 %copy-start.5 = (f32[256]{0:T(256)S(1)}, f32[256]{0:T(256)}, u32[]{:S(2)}) copy-start(f32[256]{0:T(256)} %param.17) | copy-start | bytes 3076
Sparse Core Ops, SparseCore 0:
  41.7 124.3 all-reduce.1
  257.5 9.7 reduce-scatter.1
where the time goes:
time: 307 us; the launch traced here: 306 us
  waiting for transfers between devices  126 us (41%)
  blocking collectives  116 us (38%)
  local copies, waits for them, and re-layouts  31.1 us (10%)
  between operations  13.5 us (4%)
  matrix products  7.3 us (2%)
  starting transfers between devices  7.19 us (2%)
  other arithmetic  4.24 us (1%)
    psum x1, waiting for transfers between devices, body(): projection = lax.psum(partial_proj, ('ex', 'feat'))  124 us
    all_to_all x1, blocking collectives, body(): lax.all_to_all(fetched, 'ex', split_axis=0, concat_axis=0, tiled=True)  76.2 us
    psum x1, blocking collectives, body(): lax.psum(jnp.sum(test_wide * exact_dir, axis=(0, 2)), ('ex', 'feat'))  40.1 us
    scatter x1, local copies, waits for them, and re-layouts, body(): requests = jnp.full((ex_devices, capacity), -1, jnp.int32).at[targets, sl...  18.5 us
    all_to_all x1, starting transfers between devices, body(): lax.all_to_all(requests, 'ex', split_axis=0, concat_axis=0, tiled=True)  7.11 us
  transfers between devices with their start and end apart: 3, of which 2 were waited for; matrix products, arithmetic and copies ran while one was open for 1% of the time, Pallas kernels for 0%

commit v1 on v0

--- a/solution.py
+++ b/solution.py
@@ -39,7 +39,7 @@
     exact_dir = diag_tiles[:, None, :] * test_wide + jnp.einsum(
         "afr,tr->atf", basis_tiles, scaled_proj, preferred_element_type=jnp.float32
     )
-    self_inf = lax.psum(jnp.sum(test_wide * exact_dir, axis=(0, 2)), ("ex", "feat"))
+    self_inf = lax.psum(lax.psum(jnp.sum(test_wide * exact_dir, axis=(0, 2)), "feat"), "ex")
     direction = exact_dir.astype(jnp.bfloat16)
     blocks_here = train_tiles.shape[0]
     slots_here = train_tiles.shape[1]

time: 307 us -> 304 us (level)
    psum x1 -> x2, blocking collectives: 40.1 us -> 37.1 us  [the longest x1 32.1 us: body(): lax.psum(lax.psum(jnp.sum(test_wide * exact_dir, axis=(0, 2)), 'feat'), '...]
where the time goes in v1:
time: 304 us; the launch traced here: 303 us
  waiting for transfers between devices  126 us (41%)
  blocking collectives  113 us (37%)
  local copies, waits for them, and re-layouts  31.1 us (10%)
  between operations  13.5 us (4%)
  matrix products  7.3 us (2%)
  starting transfers between devices  7.19 us (2%)
  other arithmetic  4.24 us (1%)
    psum x1, waiting for transfers between devices, body(): projection = lax.psum(partial_proj, ('ex', 'feat'))  124 us
    all_to_all x1, blocking collectives, body(): lax.all_to_all(fetched, 'ex', split_axis=0, concat_axis=0, tiled=True)  76.2 us
    psum x1, blocking collectives, body(): lax.psum(lax.psum(jnp.sum(test_wide * exact_dir, axis=(0, 2)), 'feat'), '...  32.1 us
    scatter x1, local copies, waits for them, and re-layouts, body(): requests = jnp.full((ex_devices, capacity), -1, jnp.int32).at[targets, sl...  18.5 us
    all_to_all x1, starting transfers between devices, body(): lax.all_to_all(requests, 'ex', split_axis=0, concat_axis=0, tiled=True)  7.11 us
  transfers between devices with their start and end apart: 3, of which 2 were waited for; matrix products, arithmetic and copies ran while one was open for 1% of the time, Pallas kernels for 0%

profile of v1, /device:TPU:0, one launch (start us, length us, event | category | flops | bytes accessed | tf_op | source)
XLA Modules:
  0.0 302.8 jit_solution(14479934108966226162)
XLA Ops:
  6.5 0.0 copy-start
  6.5 0.0 copy-start.4
  6.5 0.9 copy.25
  7.4 0.1 reshape.251
  7.5 0.1 reshape.250
  7.6 0.7 iota_compare_fusion.3
  8.4 0.1 lt.83
  8.5 0.1 lt.81
  8.6 0.1 fusion.11
  8.7 0.2 reduce_window_sum.11
  8.9 0.2 select_reduce_fusion
  9.1 0.6 broadcast_in_dim.15
  9.7 18.5 %scatter_fusion = s32[16,12]{1,0:T(8,128)} fusion(s32[16,12]{1,0:T(8,128)} %broadcast_in_dim.15, s32[128]{0:T(128)S(1)} %fusion.21, s32[128]{0:T(128)S(1)} %get-tuple-element.9), kind=kCustom, calls=%fused_computation.2 | custom fusion | bytes 2560 | tf_op jit(solution)/shard_map/scatter | solution.py:60
  28.2 7.1 %all-to-all-start = ((s32[16,1,12]{2,1,0:T(1,128)}), s32[16,1,12]{2,1,0:T(1,128)S(1)}, u32[]{:S(2)}, u32[]{:S(2)}) async-start(s32[16,1,12]{2,1,0:T(1,128)} %bitcast.10), calls=%async_computation | async-start | bytes 16384 | tf_op jit(solution)/shard_map/all_to_all | solution.py:63
  35.3 0.0 all-reduce.2.cloned.1.call-start
  35.4 0.7 broadcast_subtract_fusion
  36.1 0.1 copy.22
  36.2 1.6 fusion.3
  37.8 0.0 copy-done
  37.8 0.0 copy-start.1
  37.8 0.8 copy-done.1
  38.6 1.3 convolution_bitcast_fusion
  39.8 0.0 copy-start.3
  39.8 0.0 all-reduce.2.cloned.1.call-update
  39.9 0.0 reduce-scatter.2.cloned.1.call-start
  39.9 1.8 all-to-all-done
  41.7 0.1 reshape.255
  41.8 124.3 %all-reduce.2.cloned.1.call-done = f32[64,384]{1,0:T(8,128)} async-done(((f32[64,384]{1,0:T(8,128)}), f32[64,384]{1,0:T(8,128)}) %all-reduce.2.cloned.1.call-update) | async-done | bytes 98320 | tf_op jit(solution)/shard_map/psum | solution.py:37
  166.1 0.0 copy-done.4
  166.1 0.0 copy-start.2
  166.1 2.0 fusion.13
  168.2 0.0 copy-done.3
  168.2 0.0 copy-done.2
  168.2 0.8 fusion.5
  169.0 1.0 copy.28
  170.0 3.8 %gather_fusion = bf16[192,64,128]{2,1,0:T(8,128)(2,1)} fusion(bf16[32,64,128]{2,1,0:T(8,128)(2,1)} %copy.28, s32[1024]{0:T(1024)S(1)} %pad_clamp_fusion), kind=kCustom, calls=%fused_computation | custom fusion | bytes 6292224 | tf_op jit(solution)/shard_map/gather | solution.py:62
  173.8 76.2 %all_to_all.14 = bf16[16,12,64,128]{3,2,1,0:T(8,128)(2,1)} all-to-all(bf16[16,12,64,128]{3,2,1,0:T(8,128)(2,1)} %bitcast.43), channel_id=1, replica_groups=mesh['ex'=16,'feat'=2] {'ex'}, dimensions={0} | all-to-all | bytes 6291456 | tf_op jit(solution)/shard_map/all_to_all | solution.py:65
  250.0 4.2 %gather_fusion.1 = bf16[128,64,128]{2,1,0:T(8,128)(2,1)} fusion(bf16[16,12,64,128]{3,2,1,0:T(8,128)(2,1)} %all_to_all.14, s32[128]{0:T(128)S(1)} %get-tuple-element.5), kind=kCustom, calls=%fused_computation.1 | custom fusion | bytes 4195328 | tf_op jit(solution)/shard_map/gather | solution.py:67
  254.2 0.0 copy-start.5
  254.2 2.4 fusion
  256.6 0.7 copy.29
  257.3 0.0 reduce-scatter.2.cloned.1.call-update
  257.4 0.0 copy-done.5
  257.4 5.0 %psum.22 = f32[64]{0:T(128)S(1)} all-reduce(f32[64]{0:T(128)S(1)} %get-tuple-element.7), channel_id=1, replica_groups=mesh['ex'=16,'feat'=2] {'feat'}, use_global_device_ids=true, to_apply=%region_6.7 | all-reduce | flops 64 | bytes 512 | tf_op jit(solution)/shard_map/psum | solution.py:42
  262.4 32.1 %psum.23 = f32[64]{0:T(128)S(1)} all-reduce(f32[64]{0:T(128)S(1)} %psum.22), channel_id=1, replica_groups=mesh['ex'=16,'feat'=2] {'ex'}, use_global_device_ids=true, to_apply=%region_7.8 | all-reduce | flops 64 | bytes 512 | tf_op jit(solution)/shard_map/psum | solution.py:42
  294.5 0.1 dynamic-slice_sqrt_fusion
  294.6 0.0 reduce-scatter.2.cloned.1.call-done
  294.6 1.5 multiply_divide_fusion
  (6 shorter events, 0.1 us)
Async XLA Ops:
  6.5 31.2 %copy-start = (bf16[4096,384]{1,0:T(8,128)(2,1)S(1)}, bf16[4096,384]{1,0:T(8,128)(2,1)}, u32[]{:S(2)}) copy-start(bf16[4096,384]{1,0:T(8,128)(2,1)} %param.9) | copy-start | bytes 9437188
  6.5 159.6 %copy-start.4 = (f32[384]{0:T(512)S(1)}, f32[384]{0:T(512)}, u32[]{:S(2)}) copy-start(f32[384]{0:T(512)} %param.11) | copy-start | bytes 4612
  28.2 13.5 %all-to-all-start = ((s32[16,1,12]{2,1,0:T(1,128)}), s32[16,1,12]{2,1,0:T(1,128)S(1)}, u32[]{:S(2)}, u32[]{:S(2)}) async-start(s32[16,1,12]{2,1,0:T(1,128)} %bitcast.10), calls=%async_computation | async-start | bytes 16384 | tf_op jit(solution)/shard_map/all_to_all | solution.py:63
  35.3 130.8 %all-reduce.2.cloned.1.call-start = ((), (), s32[]{:S(2)}) async-start(), calls=%async_computation.3 | async-start | bytes 196608 | tf_op jit(solution)/shard_map/psum | solution.py:37
  37.8 0.8 copy-start.1
  39.8 128.4 %copy-start.3 = (f32[4096]{0:T(1024)S(1)}, f32[4096]{0:T(1024)}, u32[]{:S(2)}) copy-start(f32[4096]{0:T(1024)} %param.10) | copy-start | bytes 49156
  39.9 254.7 %reduce-scatter.2.cloned.1.call-start = ((), (), s32[]{:S(2)}) async-start(), calls=%async_computation.4 | async-start | bytes 98304 | tf_op jit(solution)/shard_map/reduce_scatter | solution.py:74
  166.1 2.1 copy-start.2
  254.2 3.1 %copy-start.5 = (f32[256]{0:T(256)S(1)}, f32[256]{0:T(256)}, u32[]{:S(2)}) copy-start(f32[256]{0:T(256)} %param.17) | copy-start | bytes 3076
Sparse Core Ops, SparseCore 0:
  41.7 124.3 all-reduce.1
  257.5 9.6 reduce-scatter.1
